TPU v7x, 256 devices: a whole 4x4x8 slice. The times are simulated.
256 devices in a mesh: pair: 32 (over z_lo, y, x), sector: 8 (over z_hi, core).
Axes of the slice: x: 4, y: 4, z: 8 (z_hi: 4, z_lo: 2; z = z_hi * 2 + z_lo), core: 2. Of those that a mesh axis runs over, the one named last changes fastest.
Arguments:
- wavefunction: float32 [8, 512, 512], P('sector', 'pair'), may hold values from -6 to 6
- preconditioner: float32 [8, 512, 512], P('sector', 'pair'), may hold values from 0.5 to 4
- left_ops: float32 [96, 8, 512, 512], P('pair', 'sector'), may hold values from -0.25 to 0.25
- right_ops: float32 [96, 8, 512, 512], P('pair', 'sector'), may hold values from -0.01953125 to 0.01953125
- charges: int32 [96], P('pair'), may hold values from 0 to 2
- coupling: int32 [8, 3], P('sector'), may hold values 0 or 1
Outputs:
- new_state: float32 [8, 512, 512], P('sector', 'pair')
- new_image: float32 [8, 512, 512], P('sector', 'pair')
- energies: float32 [2], replicated
All inputs are finite; a program needn't handle non-finite values. No bound on the sum of `coupling` on one device may be relied on, other than what follows from the above.
Results may differ from a plain program's by a relative error of at most 0.0003.
Values sent between devices are 32-bit elements; how exact they have to be, the bound alone decides.
A program may use at most 64 MiB of HBM per device.

v0:
```python
import math

import jax
import jax.numpy as jnp
from jax import lax
from jax.sharding import Mesh
from jax.sharding import PartitionSpec as P

SECTOR = ("sector_0", "sector_1")
PAIR = ("pair_0", "pair_1", "pair_2")
PAIR_SECTOR = ("pair_0", "pair_1", "pair_2", "sector_0", "sector_1")


highest = lax.Precision.HIGHEST


def shifted(block, axis, distance):
    devices = range(lax.axis_size(axis))
    route = [((i - distance) % len(devices), i) for i in devices]
    return lax.ppermute(block, axis, route)


def side_by_side(arrays, axis, dim, along):
    widths = [a.shape[along] for a in arrays]
    both = jnp.concatenate(arrays, axis=along)
    out = lax.all_gather(both, axis, axis=dim, tiled=True)
    return tuple(jnp.split(out, [sum(widths[:k]) for k in range(1, len(widths))], axis=along))


def cut_along(value, dim, peers):
    lengths = value.shape
    blocks = value.reshape(*lengths[:dim], peers, lengths[dim] // peers, *lengths[dim + 1 :])
    return jnp.moveaxis(blocks, dim, 0)


def sum_at_owner(value, axis, dim):
    peers = lax.axis_size(axis)
    blocks = lax.all_to_all(cut_along(value, dim, peers), axis, 0, 0, tiled=True)
    return jnp.sum(blocks, axis=0)


def by_axis(value, axes):
    for axis in axes:
        value = lax.psum(value, axis)
    return value


def product(first, second):
    return jnp.dot(first, second, precision=highest, preferred_element_type=jnp.float32)


def sigma_apply(vector, left_ops, right_ops, charges, coupling):
    lower_rows = shifted(vector, SECTOR, 1)
    upper_rows = shifted(vector, SECTOR, -1)
    gathered = side_by_side((lower_rows, vector, upper_rows), PAIR, 1, 0)
    stacked = jnp.concatenate(gathered, axis=0)
    own_block = stacked[1]
    targets = jnp.zeros_like(stacked)
    for which_pair in range(left_ops.shape[0]):
        left_block = left_ops[which_pair, 0]
        right_block = right_ops[which_pair, 0]
        charge_slot = charges[which_pair]
        allowed = lax.dynamic_index_in_dim(coupling[0], charge_slot, 0, keepdims=False).astype(
            jnp.float32
        )
        source_block = lax.dynamic_index_in_dim(stacked, charge_slot, 0, keepdims=False)
        forward = product(product(left_block, own_block), right_block.T)
        backward = product(product(left_block.T, source_block), right_block)
        current = lax.dynamic_index_in_dim(targets, charge_slot, 0, keepdims=False)
        targets = lax.dynamic_update_index_in_dim(
            targets, current + allowed * forward, charge_slot, 0
        )
        targets = targets.at[1].add(allowed * backward)
    from_below = shifted(targets[2], SECTOR, 1)
    from_above = shifted(targets[0], SECTOR, -1)
    combined = targets[1] + from_below + from_above
    return sum_at_owner(combined[None], PAIR, 1)


def per_device(wavefunction, preconditioner, left_ops, right_ops, charges, coupling):
    first_image = sigma_apply(wavefunction, left_ops, right_ops, charges, coupling)
    norm_sq, correlation = (
        by_axis(jnp.sum(wavefunction * wavefunction), PAIR_SECTOR),
        by_axis(jnp.sum(wavefunction * first_image), PAIR_SECTOR),
    )
    theta = correlation / norm_sq
    inverse = lax.rsqrt(norm_sq)
    vector = wavefunction * inverse
    image = first_image * inverse
    residual = image - theta * vector
    correction = residual / preconditioner
    along, squared = (
        by_axis(jnp.sum(vector * correction), PAIR_SECTOR),
        by_axis(jnp.sum(correction * correction), PAIR_SECTOR),
    )
    orthogonal = correction - along * vector
    length_sq = squared - along * along
    basis = orthogonal * lax.rsqrt(length_sq + 1e-30)
    second_image = sigma_apply(basis, left_ops, right_ops, charges, coupling)
    corner, cross = (
        by_axis(jnp.sum(basis * second_image), PAIR_SECTOR),
        by_axis(jnp.sum(vector * second_image), PAIR_SECTOR),
    )
    half = (theta - corner) / 2.0
    lowest = (theta + corner) / 2.0 - jnp.sqrt(half * half + cross * cross)
    first_weight = corner - lowest
    second_weight = -cross
    size_norm = jnp.sqrt(first_weight * first_weight + second_weight * second_weight + 1e-30)
    entries = (
        lax.axis_size(SECTOR) * lax.axis_size(PAIR) * wavefunction.shape[1] * wavefunction.shape[2]
    )
    scale = jnp.float32(math.sqrt(entries))
    factor_one = scale * first_weight / size_norm
    factor_two = scale * second_weight / size_norm
    new_state = factor_one * vector + factor_two * basis
    new_image = factor_one * image + factor_two * second_image
    energies = jnp.stack([theta, lowest])
    return (new_state, new_image, energies)


def solution(mesh):
    split = Mesh(
        mesh.devices.reshape(2, 4, 4, 4, 2), ("pair_0", "pair_1", "pair_2", "sector_0", "sector_1")
    )
    placed = (
        P(SECTOR, PAIR, None),
        P(SECTOR, PAIR, None),
        P(PAIR, SECTOR, None, None),
        P(PAIR, SECTOR, None, None),
        P(PAIR),
        P(SECTOR, None),
    )
    return jax.shard_map(
        per_device,
        mesh=split,
        in_specs=placed,
        out_specs=(P(SECTOR, PAIR, None), P(SECTOR, PAIR, None), P()),
        check_vma=False,
    )
```

profile of v0, /device:TPU:1, one launch (start us, length us, event | category | flops | bytes accessed | tf_op | source)
XLA Modules:
  0.0 650.0 jit_solution(17976514940221424542)
XLA Ops:
  28.1 128.5 %all-gather.3.cloned.1.call-done = f32[3,512,512]{2,1,0:T(8,128)} async-done(((f32[3,16,512]{2,1,0:T(8,128)}), f32[3,512,512]{2,1,0:T(8,128)}) %all-gather.3.cloned.1.call-update) | async-done | bytes 3145744 | tf_op jit(solution)/shard_map/all_gather | solution.py:26
  156.6 5.2 fusion.78
  189.0 23.1 %collective-permute-start.2 = (f32[512,512]{1,0:T(8,128)S(1)}, f32[512,512]{1,0:T(8,128)S(1)}, u32[]{:S(2)}, u32[]{:S(2)}) collective-permute-start(f32[512,512]{1,0:T(8,128)S(1)} %get-tuple-element.114), channel_id=1, source_target_pairs={{7,0},{0,1},{1,2},{2,3},{3,4},{4,5},{5,6},{6,7},{15,8},{8,9},{9,10... | collective-permute-start | bytes 3145736 | tf_op jit(solution)/shard_map/ppermute | solution.py:20
  214.0 12.9 %collective-permute-done.2 = f32[512,512]{1,0:T(8,128)S(1)} collective-permute-done((f32[512,512]{1,0:T(8,128)S(1)}, f32[512,512]{1,0:T(8,128)S(1)}, u32[]{:S(2)}, u32[]{:S(2)}) %collective-permute-start.2) | collective-permute-done | bytes 1048608 | tf_op jit(solution)/shard_map/ppermute | solution.py:20
  226.9 11.6 %collective-permute-done.3 = f32[512,512]{1,0:T(8,128)S(1)} collective-permute-done((f32[512,512]{1,0:T(8,128)S(1)}, f32[512,512]{1,0:T(8,128)S(1)}, u32[]{:S(2)}, u32[]{:S(2)}) %collective-permute-start.3) | collective-permute-done | bytes 1048608 | tf_op jit(solution)/shard_map/ppermute | solution.py:20
  240.5 21.8 %all_to_all.10 = f32[32,1,16,512]{3,2,1,0:T(8,128)} all-to-all(f32[32,1,16,512]{3,2,1,0:T(8,128)S(1)} %bitcast.225), channel_id=1, replica_groups=mesh['pair_0'=2,'pair_1'=4,'pair_2'=4,'sector_0'=4,'sector_1'=2] {'pair_..., dimensions={0} | all-to-all | bytes 2097152 | tf_op jit(solution)/shard_map/all_to_all | solution.py:38
  268.6 9.0 %all-reduce.8 = (f32[]{:T(128)}, f32[]{:T(128)}) all-reduce(f32[]{:T(128)} %get-tuple-element.109, f32[]{:T(128)} %get-tuple-element.110), channel_id=1, replica_groups=mesh['pair_0'=2,'pair_1'=4,'pair_2'=4,'sector_0'=4,'sector_1'=2] {'pair_1'}, use_global_device_ids=true, to_apply=%region_9.10 | all-reduce | flops 2 | bytes 16 | tf_op jit(solution)/shard_map/psum | solution.py:44
  277.7 7.0 %all-reduce.5 = (f32[]{:T(128)}, f32[]{:T(128)}) all-reduce(f32[]{:T(128)} %get-tuple-element.97, f32[]{:T(128)} %get-tuple-element.98), channel_id=1, replica_groups=mesh['pair_0'=2,'pair_1'=4,'pair_2'=4,'sector_0'=4,'sector_1'=2] {'pair_2'}, use_global_device_ids=true, to_apply=%region_10.11 | all-reduce | flops 2 | bytes 16 | tf_op jit(solution)/shard_map/psum | solution.py:44
  284.7 10.7 %all-reduce.2 = (f32[]{:T(128)}, f32[]{:T(128)}) all-reduce(f32[]{:T(128)} %get-tuple-element.91, f32[]{:T(128)} %get-tuple-element.92), channel_id=1, replica_groups=mesh['pair_0'=2,'pair_1'=4,'pair_2'=4,'sector_0'=4,'sector_1'=2] {'secto..., use_global_device_ids=true, to_apply=%region_11.12 | all-reduce | flops 2 | bytes 16 | tf_op jit(solution)/shard_map/psum | solution.py:44
  295.4 10.4 %all-reduce.11 = (f32[]{:T(128)}, f32[]{:T(128)}) all-reduce(f32[]{:T(128)} %get-tuple-element.85, f32[]{:T(128)} %get-tuple-element.86), channel_id=1, replica_groups=mesh['pair_0'=2,'pair_1'=4,'pair_2'=4,'sector_0'=4,'sector_1'=2] {'secto..., use_global_device_ids=true, to_apply=%region_12.13 | all-reduce | flops 2 | bytes 16 | tf_op jit(solution)/shard_map/psum | solution.py:44
  313.0 7.8 %all-reduce.7 = (f32[]{:T(128)}, f32[]{:T(128)}) all-reduce(f32[]{:T(128)} %get-tuple-element.107, f32[]{:T(128)} %get-tuple-element.108), channel_id=1, replica_groups=mesh['pair_0'=2,'pair_1'=4,'pair_2'=4,'sector_0'=4,'sector_1'=2] {'pair_1'}, use_global_device_ids=true, to_apply=%region_21.22 | all-reduce | flops 2 | bytes 16 | tf_op jit(solution)/shard_map/psum | solution.py:44
  320.9 6.7 %all-reduce.4 = (f32[]{:T(128)}, f32[]{:T(128)}) all-reduce(f32[]{:T(128)} %get-tuple-element.95, f32[]{:T(128)} %get-tuple-element.96), channel_id=1, replica_groups=mesh['pair_0'=2,'pair_1'=4,'pair_2'=4,'sector_0'=4,'sector_1'=2] {'pair_2'}, use_global_device_ids=true, to_apply=%region_22.23 | all-reduce | flops 2 | bytes 16 | tf_op jit(solution)/shard_map/psum | solution.py:44
  327.5 9.3 %all-reduce.1 = (f32[]{:T(128)}, f32[]{:T(128)}) all-reduce(f32[]{:T(128)} %get-tuple-element.89, f32[]{:T(128)} %get-tuple-element.90), channel_id=1, replica_groups=mesh['pair_0'=2,'pair_1'=4,'pair_2'=4,'sector_0'=4,'sector_1'=2] {'secto..., use_global_device_ids=true, to_apply=%region_23.24 | all-reduce | flops 2 | bytes 16 | tf_op jit(solution)/shard_map/psum | solution.py:44
  336.9 10.1 %all-reduce.10 = (f32[]{:T(128)}, f32[]{:T(128)}) all-reduce(f32[]{:T(128)} %get-tuple-element.83, f32[]{:T(128)} %get-tuple-element.84), channel_id=1, replica_groups=mesh['pair_0'=2,'pair_1'=4,'pair_2'=4,'sector_0'=4,'sector_1'=2] {'secto..., use_global_device_ids=true, to_apply=%region_24.25 | all-reduce | flops 2 | bytes 16 | tf_op jit(solution)/shard_map/psum | solution.py:44
  356.0 134.3 %all-gather.5.cloned.1.call-done = f32[3,512,512]{2,1,0:T(8,128)} async-done(((f32[3,16,512]{2,1,0:T(8,128)}), f32[3,512,512]{2,1,0:T(8,128)}) %all-gather.5.cloned.1.call-update) | async-done | bytes 3145744 | tf_op jit(solution)/shard_map/all_gather | solution.py:26
  490.2 4.8 fusion.75
  522.1 23.0 %collective-permute-start.6 = (f32[512,512]{1,0:T(8,128)S(1)}, f32[512,512]{1,0:T(8,128)S(1)}, u32[]{:S(2)}, u32[]{:S(2)}) collective-permute-start(f32[512,512]{1,0:T(8,128)S(1)} %get-tuple-element.112), channel_id=1, source_target_pairs={{7,0},{0,1},{1,2},{2,3},{3,4},{4,5},{5,6},{6,7},{15,8},{8,9},{9,10... | collective-permute-start | bytes 3145736 | tf_op jit(solution)/shard_map/ppermute | solution.py:20
  547.0 12.9 %collective-permute-done.6 = f32[512,512]{1,0:T(8,128)S(1)} collective-permute-done((f32[512,512]{1,0:T(8,128)S(1)}, f32[512,512]{1,0:T(8,128)S(1)}, u32[]{:S(2)}, u32[]{:S(2)}) %collective-permute-start.6) | collective-permute-done | bytes 1048608 | tf_op jit(solution)/shard_map/ppermute | solution.py:20
  559.9 11.6 %collective-permute-done.7 = f32[512,512]{1,0:T(8,128)S(1)} collective-permute-done((f32[512,512]{1,0:T(8,128)S(1)}, f32[512,512]{1,0:T(8,128)S(1)}, u32[]{:S(2)}, u32[]{:S(2)}) %collective-permute-start.7) | collective-permute-done | bytes 1048608 | tf_op jit(solution)/shard_map/ppermute | solution.py:20
  573.5 21.8 %all_to_all.11 = f32[32,1,16,512]{3,2,1,0:T(8,128)S(1)} all-to-all(f32[32,1,16,512]{3,2,1,0:T(8,128)S(1)} %bitcast.224), channel_id=1, replica_groups=mesh['pair_0'=2,'pair_1'=4,'pair_2'=4,'sector_0'=4,'sector_1'=2] {'pair_..., dimensions={0} | all-to-all | bytes 2097152 | tf_op jit(solution)/shard_map/all_to_all | solution.py:38
  600.4 9.0 %all-reduce.6 = (f32[]{:T(128)}, f32[]{:T(128)}) all-reduce(f32[]{:T(128)} %get-tuple-element.105, f32[]{:T(128)} %get-tuple-element.106), channel_id=1, replica_groups=mesh['pair_0'=2,'pair_1'=4,'pair_2'=4,'sector_0'=4,'sector_1'=2] {'pair_1'}, use_global_device_ids=true, to_apply=%region_34.35 | all-reduce | flops 2 | bytes 16 | tf_op jit(solution)/shard_map/psum | solution.py:44
  609.4 6.9 %all-reduce.3 = (f32[]{:T(128)}, f32[]{:T(128)}) all-reduce(f32[]{:T(128)} %get-tuple-element.93, f32[]{:T(128)} %get-tuple-element.94), channel_id=1, replica_groups=mesh['pair_0'=2,'pair_1'=4,'pair_2'=4,'sector_0'=4,'sector_1'=2] {'pair_2'}, use_global_device_ids=true, to_apply=%region_35.36 | all-reduce | flops 2 | bytes 16 | tf_op jit(solution)/shard_map/psum | solution.py:44
  616.4 10.8 %all-reduce = (f32[]{:T(128)}, f32[]{:T(128)}) all-reduce(f32[]{:T(128)} %get-tuple-element.87, f32[]{:T(128)} %get-tuple-element.88), channel_id=1, replica_groups=mesh['pair_0'=2,'pair_1'=4,'pair_2'=4,'sector_0'=4,'sector_1'=2] {'secto..., use_global_device_ids=true, to_apply=%region_36.37 | all-reduce | flops 2 | bytes 16 | tf_op jit(solution)/shard_map/psum | solution.py:44
  627.1 10.4 %all-reduce.9 = (f32[]{:T(128)}, f32[]{:T(128)}) all-reduce(f32[]{:T(128)} %get-tuple-element.81, f32[]{:T(128)} %get-tuple-element.82), channel_id=1, replica_groups=mesh['pair_0'=2,'pair_1'=4,'pair_2'=4,'sector_0'=4,'sector_1'=2] {'secto..., use_global_device_ids=true, to_apply=%region_37.38 | all-reduce | flops 2 | bytes 16 | tf_op jit(solution)/shard_map/psum | solution.py:44
  (73 shorter events, 99.6 us)
Async XLA Ops:
  7.2 149.5 %all-gather.3.cloned.1.call-start = ((), (), s32[]{:S(2)}) async-start(), calls=%async_computation.2 | async-start | bytes 3244032 | tf_op jit(solution)/shard_map/all_gather | solution.py:26
  7.2 5.8 collective-permute-start
  11.7 4.4 collective-permute-start.1
  17.5 472.7 %all-gather.5.cloned.1.call-start = ((), (), s32[]{:S(2)}) async-start(), calls=%async_computation.3 | async-start | bytes 3244032 | tf_op jit(solution)/shard_map/all_gather | solution.py:26
  156.6 5.6 copy-start.1
  161.8 3.9 copy-start
  161.8 3.9 copy-start.3
  189.0 37.9 %collective-permute-start.2 = (f32[512,512]{1,0:T(8,128)S(1)}, f32[512,512]{1,0:T(8,128)S(1)}, u32[]{:S(2)}, u32[]{:S(2)}) collective-permute-start(f32[512,512]{1,0:T(8,128)S(1)} %get-tuple-element.114), channel_id=1, source_target_pairs={{7,0},{0,1},{1,2},{2,3},{3,4},{4,5},{5,6},{6,7},{15,8},{8,9},{9,10... | collective-permute-start | bytes 3145736 | tf_op jit(solution)/shard_map/ppermute | solution.py:20
  212.0 26.4 %collective-permute-start.3 = (f32[512,512]{1,0:T(8,128)S(1)}, f32[512,512]{1,0:T(8,128)S(1)}, u32[]{:S(2)}, u32[]{:S(2)}) collective-permute-start(f32[512,512]{1,0:T(8,128)S(1)} %get-tuple-element.115), channel_id=1, source_target_pairs={{1,0},{2,1},{3,2},{4,3},{5,4},{6,5},{7,6},{0,7},{9,8},{10,9},{11,1... | collective-permute-start | bytes 3145736 | tf_op jit(solution)/shard_map/ppermute | solution.py:20
  240.4 23.1 %copy-start.5 = (f32[1,16,512]{2,1,0:T(8,128)S(1)}, f32[1,16,512]{2,1,0:T(8,128)}, u32[]{:S(2)}) copy-start(f32[1,16,512]{2,1,0:T(8,128)} %param.18) | copy-start | bytes 98308
  240.4 67.5 %copy-start.6 = (f32[1,16,512]{2,1,0:T(8,128)S(1)}, f32[1,16,512]{2,1,0:T(8,128)}, u32[]{:S(2)}) copy-start(f32[1,16,512]{2,1,0:T(8,128)} %param.19) | copy-start | bytes 98308
  349.6 2.2 collective-permute-start.4
  350.8 4.5 collective-permute-start.5
  490.2 5.3 copy-start.2
  495.1 3.9 copy-start.4
  522.1 37.8 %collective-permute-start.6 = (f32[512,512]{1,0:T(8,128)S(1)}, f32[512,512]{1,0:T(8,128)S(1)}, u32[]{:S(2)}, u32[]{:S(2)}) collective-permute-start(f32[512,512]{1,0:T(8,128)S(1)} %get-tuple-element.112), channel_id=1, source_target_pairs={{7,0},{0,1},{1,2},{2,3},{3,4},{4,5},{5,6},{6,7},{15,8},{8,9},{9,10... | collective-permute-start | bytes 3145736 | tf_op jit(solution)/shard_map/ppermute | solution.py:20
  545.1 26.4 %collective-permute-start.7 = (f32[512,512]{1,0:T(8,128)S(1)}, f32[512,512]{1,0:T(8,128)S(1)}, u32[]{:S(2)}, u32[]{:S(2)}) collective-permute-start(f32[512,512]{1,0:T(8,128)S(1)} %get-tuple-element.113), channel_id=1, source_target_pairs={{1,0},{2,1},{3,2},{4,3},{5,4},{6,5},{7,6},{0,7},{9,8},{10,9},{11,1... | collective-permute-start | bytes 3145736 | tf_op jit(solution)/shard_map/ppermute | solution.py:20
Sparse Core Ops, SparseCore 0:
  17.7 138.9 all-gather.2
  356.1 134.1 all-gather.4
where the time goes:
time: 660 us; the launch traced here: 650 us
  waiting for transfers between devices  321 us (49%)
  blocking collectives  165 us (25%)
  matrix products  70.3 us (11%)
  starting transfers between devices  51.8 us (8%)
  between operations  30.7 us (5%)
  other arithmetic  7.11 us (1%)
    all_gather x2, waiting for transfers between devices, side_by_side(): out = lax.all_gather(both, axis, axis=dim, tiled=True)  263 us
    psum x15, blocking collectives, by_axis(): value = lax.psum(value, axis)  122 us
    dot_general x24, matrix products, product(): jnp.dot(first, second, precision=highest, preferred_element_type=jnp.floa...  70.3 us
    ppermute x8, waiting for transfers between devices, shifted(): return lax.ppermute(block, axis, route)  57.9 us
    ppermute x8, starting transfers between devices, shifted(): return lax.ppermute(block, axis, route)  51.7 us
    all_to_all x2, blocking collectives, sum_at_owner(): lax.all_to_all(cut_along(value, dim, peers), axis, 0, 0, tiled=True)  43.6 us
  transfers between devices with their start and end apart: 10, of which 10 were waited for; matrix products, arithmetic and copies ran while one was open for 1% of the time, Pallas kernels for 0%

commit v1 on v0

v1 whole, which is shorter than its diff:
```python
import math

import jax
import jax.numpy as jnp
from jax import lax
from jax.experimental import pallas as pl
from jax.experimental.pallas import tpu as pltpu
from jax.sharding import Mesh
from jax.sharding import PartitionSpec as P

SECTOR = ("zh", "core")
PAIR = ("zl", "y", "x")
MESH = pl.DeviceIdType.MESH
F32 = jnp.float32
BF16 = jnp.bfloat16

M = 512
ROWS = 16
PAIRS = 3
OUTER, OWN, OTHER = 0, 1, 2
WAVES = 2
CW = M // WAVES
TILE = (8, 128)


def split(x):
    high = x.astype(BF16)
    return high, (x - high.astype(F32)).astype(BF16)


def total(x):
    return jnp.sum(jnp.sum(x, axis=0, keepdims=True), axis=1, keepdims=True)


def dot(a, b):
    return jnp.dot(a, b, preferred_element_type=F32)


def kernel(
    charges,
    coupling,
    w_in,
    pre_in,
    l_hbm,
    r_hbm,
    state_out,
    image_out,
    energy_out,
    raw,
    lcat,
    ltcat,
    rcat,
    rtcat,
    v,
    vcat,
    ycat,
    zcat,
    fbuf,
    tsum,
    otherbuf,
    bulk_half,
    bulk_full,
    tail_half,
    tail_full,
    zbuf,
    image,
    corrected,
    arbuf,
    load_sem,
    z_s,
    z_r,
    ring_s,
    ring_r,
    other_s,
    other_r,
    rz_s,
    rz_r,
    rring_s,
    rring_r,
    rother_s,
    rother_r,
    ar_s,
    ar_r,
):
    zl, y, x = (lax.axis_index(a) for a in PAIR)
    zh, core = (lax.axis_index(a) for a in SECTOR)
    far = lax.rem(zh + 2 * core + 3, 4)
    plane, line = y * 4 + x, zl * 8 + zh * 2 + core

    def plane_peer(d):
        peer = lax.rem(plane + d, 16)
        return {"y": peer // 4, "x": lax.rem(peer, 4)}

    def line_peer(d):
        peer = lax.rem(line + d, 16)
        return {"zl": peer // 8, "zh": lax.rem(peer // 2, 4), "core": lax.rem(peer, 2)}

    peers = (plane_peer, line_peer)
    places = (plane, line)

    def copy(src, dst, send, recv, device):
        return pltpu.make_async_remote_copy(
            src_ref=src,
            dst_ref=dst,
            send_sem=send,
            recv_sem=recv,
            device_id=device,
            device_id_type=MESH,
        )

    loads = []
    for p in range(PAIRS):
        loads.append(
            (
                pltpu.make_async_copy(l_hbm.at[p], raw.at[0, p], load_sem.at[0, p]),
                pltpu.make_async_copy(r_hbm.at[p], raw.at[1, p], load_sem.at[1, p]),
            )
        )
        for c in loads[-1]:
            c.start()

    barrier = pltpu.get_barrier_semaphore()

    @pl.loop(1, 16)
    def _(d):
        pl.semaphore_signal(barrier, inc=1, device_id=plane_peer(d), device_id_type=MESH)
        pl.semaphore_signal(barrier, inc=1, device_id=line_peer(d), device_id_type=MESH)

    pl.semaphore_wait(barrier, 30)

    roles, weights = [], []
    for p in range(PAIRS):
        charge = charges[p]
        roles.append(jnp.where(core == 0, charge, 2 - charge))
        weights.append(coupling[0, charge].astype(F32))

    def gathering(app):
        block = v.at[app]
        sends = []

        def unit_of(role, wave):
            cols = pl.ds(wave * CW, CW)
            if role == OUTER:
                first = lambda i, h: block.at[role, h, y, i, :, cols]
                second = lambda i, h: block.at[role, h, i, :, :, cols]
                return (("x", x, first), ("y", y, second))
            first = lambda i, h: block.at[role, h, i, x, :, cols]
            second = lambda i, h: block.at[role, h, :, i, :, cols]
            return (("y", y, first), ("x", x, second))

        def ring(role, wave, phase):
            axis, i, unit = unit_of(role, wave)[phase]
            right, left = lax.rem(i + 1, 4), lax.rem(i + 3, 4)
            send, recv = ring_s.at[wave, role, phase], ring_r.at[wave, role, phase]

            def mk(ref, device, k):
                return copy(ref, ref, send.at[k], recv.at[k], {axis: device})

            first = [
                mk(unit(i, 0), right, 0),
                mk(unit(i, 1), left, 1),
                mk(unit(i, 1), right, 2),
                mk(unit(i, 0), left, 3),
            ]
            onward = [mk(unit(left, 0), right, 4), mk(unit(right, 1), left, 5)]
            return first, onward

        def wave_steps(wave):
            cols = pl.ds(wave * CW, CW)
            mine = block.at[OWN, zl, y, x, :, cols]
            zc = [copy(mine, mine, z_s.at[wave, 0], z_r.at[wave, 0], {"zl": 1 - zl})]
            for q in range(2):
                zc.append(
                    copy(
                        mine,
                        block.at[OUTER, zl, y, x, :, cols],
                        z_s.at[wave, 1 + q],
                        z_r.at[wave, 1 + zl],
                        {"zl": q, "zh": far, "core": 1 - core},
                    )
                )
            rings = [[ring(r, wave, ph) for r in (OUTER, OWN)] for ph in range(2)]
            onto = copy(
                block.at[OWN, :, :, :, :, cols],
                block.at[OTHER, :, :, :, :, cols],
                other_s.at[wave],
                other_r.at[wave],
                {"core": 1 - core},
            )

            def s0():
                for c in zc:
                    c.start()
                sends.extend(zc)

            def start(phase):
                for k in range(4):
                    for first, _ in rings[phase]:
                        first[k].start()
                        sends.append(first[k])

            def onward(phase):
                for k in range(2):
                    for first, fwd in rings[phase]:
                        first[k].wait_recv()
                        fwd[k].start()
                        sends.append(fwd[k])

            def finish(phase, which):
                first, fwd = rings[phase][which]
                for c in (first[2], first[3], fwd[0], fwd[1]):
                    c.wait_recv()

            def s1():
                zc[0].wait_recv()
                for q in range(2):
                    there = block.at[OUTER, q, y, x, :, cols]
                    copy(
                        there, there, z_s.at[wave, 1 + q], z_r.at[wave, 1 + q], {"zl": 1 - zl}
                    ).wait_recv()
                start(0)

            def s3():
                finish(0, 0)
                finish(0, 1)
                start(1)

            def s5():
                finish(1, 1)
                onto.start()
                sends.append(onto)

            def s6():
                finish(1, 0)

            return [s0, s1, lambda: onward(0), s3, lambda: onward(1), s5, s6, onto.wait_recv]

        return [wave_steps(w) for w in range(WAVES)], sends

    def summing(app):
        sends = []

        def pieces(role, wave):
            cols = pl.ds(wave * CW, CW)
            if role == OUTER:
                first = lambda d, h: tsum.at[role, h, d, :, :, cols]
                second = lambda d, h: tsum.at[role, h, y, d, :, cols]
                return (("y", y, first), ("x", x, second))
            first = lambda d, h: tsum.at[role, h, :, d, :, cols]
            second = lambda d, h: tsum.at[role, h, d, x, :, cols]
            return (("x", x, first), ("y", y, second))

        def ring(role, wave, phase):
            axis, i, chunk = pieces(role, wave)[phase]
            right, left, opposite = lax.rem(i + 1, 4), lax.rem(i + 3, 4), lax.rem(i + 2, 4)
            send, recv = rring_s.at[wave, role, phase], rring_r.at[wave, role, phase]
            half = (bulk_half, tail_half)[phase].at[wave, role]
            full = (bulk_full, tail_full)[phase].at[wave, role]

            def mk(src, dst, device, k):
                return copy(src, dst, send.at[k], recv.at[k], {axis: device})

            first = [
                mk(chunk(opposite, 0), half.at[0], right, 0),
                mk(chunk(opposite, 1), half.at[1], left, 1),
                mk(chunk(right, 1), full.at[0, 1], right, 2),
                mk(chunk(left, 0), full.at[1, 0], left, 3),
            ]
            onward = [
                mk(chunk(right, 0), full.at[0, 0], right, 4),
                mk(chunk(left, 1), full.at[1, 1], left, 5),
            ]

            def pass_on(k):
                first[k].wait_recv()
                mine = chunk(right, 0) if k == 0 else chunk(left, 1)
                mine[...] += half[k]
                onward[k].start()
                sends.append(onward[k])

            def finish():
                for c in (first[2], first[3], onward[0], onward[1]):
                    c.wait_recv()
                for h in range(2):
                    mine = chunk(i, h)
                    mine[...] += full[0, h] + full[1, h]

            return first, pass_on, finish

        def wave_steps(wave):
            cols = pl.ds(wave * CW, CW)
            rings = [[ring(r, wave, ph) for r in (OUTER, OWN)] for ph in range(2)]
            onto = copy(
                tsum.at[OTHER, :, :, :, :, cols],
                otherbuf.at[wave],
                rother_s.at[wave],
                rother_r.at[wave],
                {"core": 1 - core},
            )
            zc = [
                copy(
                    tsum.at[OWN, 1 - zl, y, x, :, cols],
                    zbuf.at[wave, 0],
                    rz_s.at[wave, 0],
                    rz_r.at[wave, 0],
                    {"zl": 1 - zl},
                )
            ]
            for q in range(2):
                zc.append(
                    copy(
                        tsum.at[OUTER, q, y, x, :, cols],
                        zbuf.at[wave, 1 + zl],
                        rz_s.at[wave, 1 + q],
                        rz_r.at[wave, 1 + zl],
                        {"zl": q, "zh": far, "core": 1 - core},
                    )
                )

            def start(phase, which):
                for c in rings[phase][which][0]:
                    c.start()
                    sends.append(c)

            def pass_on(phase):
                for k in range(2):
                    for r in rings[phase]:
                        r[1](k)

            def give_other():
                onto.start()
                sends.append(onto)

            def middle():
                rings[0][0][2]()
                start(1, 0)
                rings[0][1][2]()
                start(1, 1)

            def last():
                rings[1][0][2]()
                rings[1][1][2]()
                for c in zc:
                    c.start()
                sends.extend(zc)

            def collect():
                zc[0].wait_recv()
                for q in range(2):
                    copy(
                        tsum.at[OUTER, q, y, x, :, cols],
                        zbuf.at[wave, 1 + q],
                        rz_s.at[wave, 1 + q],
                        rz_r.at[wave, 1 + q],
                        {"zl": 1 - zl},
                    ).wait_recv()
                image[:, cols] = (tsum[OWN, zl, y, x, :, cols] + zbuf[wave, 0]) + (
                    zbuf[wave, 1] + zbuf[wave, 2]
                )

            return {
                "outer": lambda: start(0, 0),
                "own": lambda: start(0, 1),
                "other": give_other,
                "take": onto.wait_recv,
                "steps": [
                    lambda: pass_on(0),
                    middle,
                    lambda: pass_on(1),
                    last,
                    collect,
                ],
            }

        return [wave_steps(w) for w in range(WAVES)], sends

    def reduction(k, stage, tile):
        place = places[stage]
        buf = arbuf.at[k, stage]
        buf[place] = tile

        def one(d):
            mine = buf.at[place]
            return copy(mine, mine, ar_s.at[k, stage], ar_r.at[k, stage], peers[stage](d))

        @pl.loop(1, 16)
        def _(d):
            one(d).start()

        def finish():
            many = buf.at[pl.ds(0, 15)]
            waited = copy(many, many, ar_s.at[k, stage], ar_r.at[k, stage], peers[stage](1))
            waited.wait_recv()
            waited.wait_send()
            return jnp.sum(buf[...], axis=0)

        return finish

    def packed(*values):
        row = lax.broadcasted_iota(jnp.int32, TILE, 0)
        tile = jnp.zeros(TILE, F32)
        for k, value in enumerate(values):
            tile = jnp.where(row == k, value, tile)
        return tile

    def prepare():
        for p in range(PAIRS):
            for c in loads[p]:
                c.wait()

        @pl.loop(0, PAIRS * 4)
        def _(step):
            p = step // 4
            at = pl.multiple_of(lax.rem(step, 4) * 128, 128)
            at2 = pl.multiple_of(at + M, 128)
            at3 = pl.multiple_of(at + 2 * M, 128)
            rows = pl.ds(at, 128)
            left_rows, right_rows = raw[0, p, rows, :], raw[1, p, rows, :]
            hi, lo = split(left_rows)
            lcat[p, rows, 0:M] = hi
            lcat[p, rows, M : 2 * M] = hi
            lcat[p, rows, 2 * M :] = lo
            hi, lo = split(left_rows.T)
            ltcat[p, :, rows] = hi
            ltcat[p, :, pl.ds(at2, 128)] = hi
            ltcat[p, :, pl.ds(at3, 128)] = lo
            hi, lo = split(right_rows)
            rcat[p, rows, :] = hi
            rcat[p, pl.ds(at2, 128), :] = hi
            rcat[p, pl.ds(at3, 128), :] = lo
            hi, lo = split(right_rows.T)
            for third, part in enumerate((hi, hi, lo)):
                rtcat[p, third * M : (third + 1) * M, rows] = part

    def halve(app, role, wave):
        cols = pl.ds(wave * CW, CW)

        @pl.loop(0, 8)
        def _(step):
            h, j = step // 4, lax.rem(step, 4)
            at = pl.multiple_of(step * 64, 64)
            hi, lo = split(v[app, role, h, j, :, :, cols].reshape(64, CW))
            vcat[role, pl.ds(at, 64), cols] = hi
            vcat[role, pl.ds(pl.multiple_of(at + M, 64), 64), cols] = lo
            vcat[role, pl.ds(pl.multiple_of(at + 2 * M, 64), 64), cols] = hi

    def first_products(wave, forward):
        cols = pl.ds(wave * CW, CW)
        for p in range(PAIRS):
            if forward:
                hi, lo = split(dot(lcat[p], vcat[OWN, :, cols]))
                into = ycat
            else:
                hi, lo = split(weights[p] * dot(ltcat[p], vcat[roles[p], :, cols]))
                into = zcat
            for third, part in enumerate((hi, lo, hi)):
                into[p, :, third * M + wave * CW : third * M + (wave + 1) * CW] = part

    def forward_terms(app, wave):
        cols = pl.ds(wave * CW, CW)
        for p in range(PAIRS):
            fbuf[p] = dot(ycat[p], rtcat[p, :, cols])
        factors = [
            [jnp.where(roles[p] == r, weights[p], 0.0) for p in range(PAIRS)] for r in range(3)
        ]

        def body(step, acc):
            h, j = step // 4, lax.rem(step, 4)
            rows = pl.ds(pl.multiple_of(step * 64, 64), 64)
            f = [fbuf[p, rows, :] for p in range(PAIRS)]
            for r in range(3):
                term = factors[r][0] * f[0] + factors[r][1] * f[1] + factors[r][2] * f[2]
                tsum[r, h, j, :, :, cols] = term.reshape(4, ROWS, CW)
                both = term * v[app, r, h, j, :, :, cols].reshape(64, CW)
                acc = acc + jnp.sum(both.reshape(8, 8, CW), axis=0)
            return acc

        return lax.fori_loop(0, 8, body, jnp.zeros((8, CW), F32))

    def backward_terms(wave):
        cols = pl.ds(wave * CW, CW)
        for p in range(PAIRS):
            fbuf[p] = dot(zcat[p], rcat[p, :, cols])

    def join(wave):
        cols = pl.ds(wave * CW, CW)

        @pl.loop(0, 8)
        def _(step):
            h, j = step // 4, lax.rem(step, 4)
            rows = pl.ds(pl.multiple_of(step * 64, 64), 64)
            back = fbuf[0, rows, :] + fbuf[1, rows, :] + fbuf[2, rows, :]
            tsum[OWN, h, j, :, :, cols] += (
                back.reshape(4, ROWS, CW) + otherbuf[wave, h, j]
            )

    def apply(app, source, before, extra):
        v[app, OWN, zl, y, x] = source
        waves, gather_sends = gathering(app)
        for k in range(2):
            for steps in waves:
                steps[k]()
            if k == 0:
                before()
        for k in range(2, 8):
            for w, steps in enumerate(waves):
                steps[k]()
        for w in range(WAVES):
            for r in range(3):
                halve(app, r, w)
            first_products(w, True)
            first_products(w, False)
        waves, sum_sends = summing(app)
        parts = []
        for w, steps in enumerate(waves):
            parts.append(forward_terms(app, w))
            steps["other"]()
            steps["outer"]()
            backward_terms(w)
            steps["take"]()
            join(w)
            steps["own"]()
        partial = 2.0 * sum(total(part) for part in parts)
        finish = extra(partial)
        for k in range(5):
            for steps in waves:
                steps["steps"][k]()
            if k == 1:
                finish = reduction(2 * app, 1, finish())
        for c in gather_sends + sum_sends:
            c.wait_send()
        return finish()

    w = w_in[...]
    norm_part = total(w * w)
    sums = apply(0, w, prepare, lambda part: reduction(0, 0, packed(norm_part, part)))
    norm_sq, correlation = sums[0:1, 0:1], sums[1:2, 0:1]
    theta = correlation / norm_sq
    inverse = lax.rsqrt(norm_sq)
    vector = w * inverse
    first = image[...] * inverse
    correction = (first - theta * vector) / pre_in[...]
    corrected[...] = correction
    image_out[...] = first
    finish = reduction(
        1,
        0,
        packed(
            total(vector * correction), total(correction * correction), total(first * correction)
        ),
    )
    held = []

    def second_extra(part):
        held.append(reduction(1, 1, finish()))
        return reduction(2, 0, packed(part))

    sums = apply(1, correction, lambda: None, second_extra)
    product = sums[0:1, 0:1]
    sums = held[0]()
    along, squared, with_image = sums[0:1, 0:1], sums[1:2, 0:1], sums[2:3, 0:1]
    length_sq = squared - along * along
    scale_back = lax.rsqrt(length_sq + 1e-30)
    corner = (
        scale_back * scale_back * (product - 2.0 * along * with_image + along * along * theta)
    )
    cross = scale_back * (with_image - along * theta)
    half = (theta - corner) / 2.0
    lowest = (theta + corner) / 2.0 - jnp.sqrt(half * half + cross * cross)
    u1 = corner - lowest
    u2 = -cross
    size_norm = jnp.sqrt(u1 * u1 + u2 * u2 + 1e-30)
    scale = math.sqrt(8 * M * M)
    one, two = scale * u1 / size_norm, scale * u2 / size_norm
    vector = w_in[...] * inverse
    first = image_out[...]
    basis = (corrected[...] - along * vector) * scale_back
    second = (image[...] - along * first) * scale_back
    state_out[...] = one * vector + two * basis
    image_out[...] = one * first + two * second
    energy_out[...] = packed(theta, lowest)


def per_device(wavefunction, preconditioner, left_ops, right_ops, charges, coupling):
    rows = jax.ShapeDtypeStruct((ROWS, M), F32)
    vmem = pl.BlockSpec(memory_space=pltpu.VMEM)
    smem = pl.BlockSpec(memory_space=pltpu.SMEM)
    dma = pltpu.SemaphoreType.DMA
    state, image, energies = pl.pallas_call(
        kernel,
        out_shape=(rows, rows, jax.ShapeDtypeStruct(TILE, F32)),
        in_specs=[smem, smem, vmem, vmem]
        + [pl.BlockSpec(memory_space=pl.ANY)] * 2,
        out_specs=(vmem, vmem, vmem),
        scratch_shapes=[
            pltpu.VMEM((2, PAIRS, M, M), F32),
            pltpu.VMEM((PAIRS, M, 3 * M), BF16),
            pltpu.VMEM((PAIRS, M, 3 * M), BF16),
            pltpu.VMEM((PAIRS, 3 * M, M), BF16),
            pltpu.VMEM((PAIRS, 3 * M, M), BF16),
            pltpu.VMEM((2, 3, 2, 4, 4, ROWS, M), F32),
            pltpu.VMEM((3, 3 * M, M), BF16),
            pltpu.VMEM((PAIRS, M, 3 * M), BF16),
            pltpu.VMEM((PAIRS, M, 3 * M), BF16),
            pltpu.VMEM((PAIRS, M, CW), F32),
            pltpu.VMEM((3, 2, 4, 4, ROWS, M), F32),
            pltpu.VMEM((WAVES, 2, 4, 4, ROWS, CW), F32),
            pltpu.VMEM((WAVES, 2, 2, 4, ROWS, CW), F32),
            pltpu.VMEM((WAVES, 2, 2, 2, 4, ROWS, CW), F32),
            pltpu.VMEM((WAVES, 2, 2, ROWS, CW), F32),
            pltpu.VMEM((WAVES, 2, 2, 2, ROWS, CW), F32),
            pltpu.VMEM((WAVES, 3, ROWS, CW), F32),
            pltpu.VMEM((ROWS, M), F32),
            pltpu.VMEM((ROWS, M), F32),
            pltpu.VMEM((3, 2, 16) + TILE, F32),
            dma((2, PAIRS)),
            dma((WAVES, 3)),
            dma((WAVES, 3)),
            dma((WAVES, 2, 2, 6)),
            dma((WAVES, 2, 2, 6)),
            dma((WAVES,)),
            dma((WAVES,)),
            dma((WAVES, 3)),
            dma((WAVES, 3)),
            dma((WAVES, 2, 2, 6)),
            dma((WAVES, 2, 2, 6)),
            dma((WAVES,)),
            dma((WAVES,)),
            dma((3, 2)),
            dma((3, 2)),
        ],
        compiler_params=pltpu.CompilerParams(
            collective_id=0, has_side_effects=True, vmem_limit_bytes=60 * 1024 * 1024
        ),
    )(
        charges,
        coupling,
        wavefunction.reshape(ROWS, M),
        preconditioner.reshape(ROWS, M),
        left_ops.reshape(PAIRS, M, M),
        right_ops.reshape(PAIRS, M, M),
    )
    return state.reshape(1, ROWS, M), image.reshape(1, ROWS, M), energies[0:2, 0]


def solution(mesh):
    split_mesh = Mesh(mesh.devices.reshape(2, 4, 4, 4, 2), PAIR + SECTOR)
    placed = (
        P(SECTOR, PAIR, None),
        P(SECTOR, PAIR, None),
        P(PAIR, SECTOR, None, None),
        P(PAIR, SECTOR, None, None),
        P(PAIR),
        P(SECTOR, None),
    )
    return jax.shard_map(
        per_device,
        mesh=split_mesh,
        in_specs=placed,
        out_specs=(P(SECTOR, PAIR, None), P(SECTOR, PAIR, None), P()),
        check_vma=False,
    )
```

time: 660 us -> 135 us (0.20); the launches traced: 650 us -> 134 us
  waiting for transfers between devices: 321 us -> 0 us
  blocking collectives: 165 us -> 0 us
  Pallas kernels: 0 us -> 130 us
  matrix products: 70.3 us -> 0 us
  starting transfers between devices: 51.8 us -> 0 us
  between operations: 30.7 us -> 0.64 us
  other arithmetic: 7.11 us -> 0 us
    all_gather x2 -> x0, waiting for transfers between devices: 263 us -> none  [side_by_side(): out = lax.all_gather(both, axis, axis=dim, tiled=True)]
    pallas_call x0 -> x1, Pallas kernels: none -> 130 us  [per_device(): pl.pallas_call(kernel, out_shape=(rows, rows, jax.ShapeDtypeStruct(TILE,...]
    psum x15 -> x0, blocking collectives: 122 us -> none  [by_axis(): value = lax.psum(value, axis)]
    dot_general x24 -> x0, matrix products: 70.3 us -> none  [product(): jnp.dot(first, second, precision=highest, preferred_element_type=jnp.floa...]
    ppermute x8 -> x0, waiting for transfers between devices: 57.9 us -> none  [shifted(): return lax.ppermute(block, axis, route)]
    ppermute x8 -> x0, starting transfers between devices: 51.7 us -> none  [shifted(): return lax.ppermute(block, axis, route)]
    all_to_all x2 -> x0, blocking collectives: 43.6 us -> none  [sum_at_owner(): lax.all_to_all(cut_along(value, dim, peers), axis, 0, 0, tiled=True)]
  transfers between devices with their start and end apart: 10 -> 0, of which waited for: 10 -> 0; matrix products, arithmetic and copies ran while one was open for 1% -> 0% of each run, Pallas kernels for 0% -> 0%
where the time goes in v1:
time: 135 us; the launch traced here: 134 us
  Pallas kernels  130 us (96%)
  local copies, waits for them, and re-layouts  4.05 us (3%)
    pallas_call x1, Pallas kernels, per_device(): pl.pallas_call(kernel, out_shape=(rows, rows, jax.ShapeDtypeStruct(TILE,...  130 us
    unnamed x2, local copies, waits for them, and re-layouts  2.75 us

profile of v1, /device:TPU:1, one launch (start us, length us, event | category | flops | bytes accessed | tf_op | source)
XLA Modules:
  0.0 134.2 jit_solution(15905503937651304469)
XLA Ops:
  0.6 129.5 %shard_map.85 = (f32[16,512]{1,0:T(8,128)}, f32[16,512]{1,0:T(8,128)}, f32[8,128]{1,0:T(8,128)}) custom-call(s32[3]{0:T(128)} %charges.1, s32[1,3]{1,0:T(1,128)} %coupling.1, f32[16,512]{1,0:T(8,128)} %bitcast.8, f32[16,512]{1,0:T(8,128)} %bitcast.9, f32[3,512,512]{2,1,0:T(8,128)} %bitcast.6, f32[3,512,512]{2,1,0:T(8,128)} %bitcast.7), custom_call_target="tpu_custom_call" | custom-call | tf_op jit(solution)/shard_map/pallas_call | solution.py:589
  130.2 1.3 slice_reduce_fusion
  131.5 1.4 %copy.11 = f32[1,16,512]{2,1,0:T(8,128)} copy(f32[1,16,512]{2,1,0:T(8,128)} %bitcast.11) | data formatting | bytes 65536
  132.9 1.4 %copy.12 = f32[1,16,512]{2,1,0:T(8,128)} copy(f32[1,16,512]{2,1,0:T(8,128)} %bitcast.10) | data formatting | bytes 65536

commit v2 on v1

v2 whole, which is shorter than its diff:
```python
import math

import jax
import jax.numpy as jnp
from jax import lax
from jax.experimental import pallas as pl
from jax.experimental.pallas import tpu as pltpu
from jax.sharding import Mesh
from jax.sharding import PartitionSpec as P

SECTOR = ("zh", "core")
PAIR = ("zl", "y", "x")
MESH = pl.DeviceIdType.MESH
F32 = jnp.float32
BF16 = jnp.bfloat16

M = 512
ROWS = 16
PAIRS = 3
OUTER, OWN, OTHER = 0, 1, 2
WAVES = 2
CW = M // WAVES
TILE = (8, 128)


def split(x):
    high = x.astype(BF16)
    return high, (x - high.astype(F32)).astype(BF16)


def total(x):
    return jnp.sum(jnp.sum(x, axis=0, keepdims=True), axis=1, keepdims=True)


def dot(a, b):
    return jnp.dot(a, b, preferred_element_type=F32)


def kernel(
    charges,
    coupling,
    w_in,
    pre_in,
    l_hbm,
    r_hbm,
    packed_out,
    raw,
    lcat,
    ltcat,
    rcat,
    rtcat,
    v,
    vcat,
    ycat,
    zcat,
    fbuf,
    tsum,
    otherbuf,
    bulk_half,
    bulk_full,
    tail3,
    tail7,
    tail2,
    image,
    corrected,
    held,
    arbuf,
    load_sem,
    z_s,
    z_r,
    ring_s,
    ring_r,
    other_s,
    other_r,
    rz_s,
    rz_r,
    rring_s,
    rring_r,
    rother_s,
    rother_r,
    ar_s,
    ar_r,
):
    zl, y, x = (lax.axis_index(a) for a in PAIR)
    zh, core = (lax.axis_index(a) for a in SECTOR)
    far = lax.rem(zh + 2 * core + 3, 4)
    places = (x, zl * 4 + y, zh * 2 + core)
    sizes = (4, 8, 8)

    def along_x(d):
        return {"x": lax.rem(x + d, 4)}

    def along_y(d):
        return {"y": lax.rem(y + d, 4)}

    def along_yz(d):
        place = lax.rem(places[1] + d, 8)
        return {"zl": place // 4, "y": lax.rem(place, 4)}

    def along_sector(d):
        place = lax.rem(places[2] + d, 8)
        return {"zh": place // 2, "core": lax.rem(place, 2)}

    peers = (along_x, along_yz, along_sector)

    def copy(src, dst, send, recv, device):
        return pltpu.make_async_remote_copy(
            src_ref=src,
            dst_ref=dst,
            send_sem=send,
            recv_sem=recv,
            device_id=device,
            device_id_type=MESH,
        )

    loads = []
    for p in range(PAIRS):
        loads.append(
            (
                pltpu.make_async_copy(l_hbm.at[p], raw.at[0, p], load_sem.at[0, p]),
                pltpu.make_async_copy(r_hbm.at[p], raw.at[1, p], load_sem.at[1, p]),
            )
        )
        for c in loads[-1]:
            c.start()

    barrier = pltpu.get_barrier_semaphore()
    signals = [g(d) for g, n in zip(peers, sizes) for d in range(1, n)]
    signals.append({"zl": 1 - zl, "zh": far, "core": 1 - core})
    for device in signals:
        pl.semaphore_signal(barrier, inc=1, device_id=device, device_id_type=MESH)

    roles, weights = [], []
    for p in range(PAIRS):
        charge = charges[p]
        roles.append(jnp.where(core == 0, charge, 2 - charge))
        weights.append(coupling[0, charge].astype(F32))

    def gathering(app):
        block = v.at[app]
        sends = []

        def begin(copies):
            for c in copies:
                c.start()
            sends.extend(copies)

        def wave_steps(wave):
            cols = pl.ds(wave * CW, CW)
            mine = block.at[OWN, zl, y, x, :, cols]

            def ring(phase, ref, group, n):
                return [
                    copy(
                        ref,
                        ref,
                        ring_s.at[wave, phase, d - 1],
                        ring_r.at[wave, phase, d - 1],
                        group(d),
                    )
                    for d in range(1, n)
                ]

            across = [
                copy(
                    mine,
                    block.at[OUTER, zl, y, x, :, cols],
                    z_s.at[wave, q],
                    z_r.at[wave, zl],
                    {"zl": q, "zh": far, "core": 1 - core},
                )
                for q in range(2)
            ]
            own1 = ring(0, mine, along_yz, 8)
            outer1 = ring(2, block.at[OUTER, :, y, x, :, cols], along_x, 4)

            def two_way(phase, unit, i, group):
                def one(ref, d, k):
                    return copy(
                        ref, ref, ring_s.at[wave, phase, k], ring_r.at[wave, phase, k], group(d)
                    )

                first = [
                    one(unit(i, 0), 1, 0),
                    one(unit(i, 1), 3, 1),
                    one(unit(i, 1), 1, 2),
                    one(unit(i, 0), 3, 3),
                ]
                onward = [
                    one(unit(lax.rem(i + 3, 4), 0), 1, 4),
                    one(unit(lax.rem(i + 1, 4), 1), 3, 5),
                ]
                return first, onward

            own2, own2_on = two_way(1, lambda i, h: block.at[OWN, h, :, i, :, cols], x, along_x)
            outer2, outer2_on = two_way(
                3, lambda i, h: block.at[OUTER, h, i, :, :, cols], y, along_y
            )
            onto = copy(
                block.at[OWN, :, :, :, :, cols],
                block.at[OTHER, :, :, :, :, cols],
                other_s.at[wave],
                other_r.at[wave],
                {"core": 1 - core},
            )

            def arrived(copies):
                for c in copies:
                    c.wait_recv()

            def outer_first():
                for q in range(2):
                    there = block.at[OUTER, q, y, x, :, cols]
                    copy(
                        there, there, z_s.at[wave, q], z_r.at[wave, q], {"zl": 1 - zl}
                    ).wait_recv()
                begin(outer1)

            def own_second():
                arrived(own1)
                begin(own2)

            def outer_second():
                arrived(outer1)
                begin(outer2)

            def pass_on(first, onward):
                for k in range(2):
                    first[k].wait_recv()
                    begin([onward[k]])

            def hand_over():
                arrived(own2[2:] + own2_on)
                begin([onto])

            return {
                "across": lambda: begin(across),
                "own1": lambda: begin(own1),
                "outer1": outer_first,
                "own2": own_second,
                "outer2": outer_second,
                "own": hand_over,
                "own2_on": lambda: pass_on(own2, own2_on),
                "outer2_on": lambda: pass_on(outer2, outer2_on),
                "outer": lambda: arrived(outer2[2:] + outer2_on),
                "other": onto.wait_recv,
            }

        return [wave_steps(w) for w in range(WAVES)], sends

    def summing(app):
        sends = []

        def begin(copies):
            for c in copies:
                c.start()
            sends.extend(copies)

        def arrived(copies):
            for c in copies:
                c.wait_recv()

        def wave_steps(wave):
            cols = pl.ds(wave * CW, CW)

            def ring(phase, chunk, into, group, n):
                return [
                    copy(
                        chunk(d),
                        into.at[d - 1],
                        rring_s.at[wave, phase, d - 1],
                        rring_r.at[wave, phase, d - 1],
                        group(d),
                    )
                    for d in range(1, n)
                ]

            small_outer, small_own, crossed = tail3.at[wave], tail7.at[wave], tail2.at[wave]
            def two_way(phase, chunk, half, full, i, group):
                def one(src, dst, d, k):
                    return copy(
                        src, dst, rring_s.at[wave, phase, k], rring_r.at[wave, phase, k], group(d)
                    )

                right, left, opposite = lax.rem(i + 1, 4), lax.rem(i + 3, 4), lax.rem(i + 2, 4)
                first = [
                    one(chunk(opposite, 0), half.at[0], 1, 0),
                    one(chunk(opposite, 1), half.at[1], 3, 1),
                    one(chunk(right, 1), full.at[0, 1], 1, 2),
                    one(chunk(left, 0), full.at[1, 0], 3, 3),
                ]
                onward = [
                    one(chunk(right, 0), full.at[0, 0], 1, 4),
                    one(chunk(left, 1), full.at[1, 1], 3, 5),
                ]

                def pass_on():
                    for k, mine in enumerate((chunk(right, 0), chunk(left, 1))):
                        first[k].wait_recv()
                        mine[...] += half[k]
                        begin([onward[k]])

                def finish():
                    arrived(first[2:] + onward)
                    for h in range(2):
                        mine = chunk(i, h)
                        mine[...] += full[0, h] + full[1, h]

                return first, pass_on, finish

            outer2, outer2_on, outer2_end = two_way(
                0,
                lambda d, h: tsum.at[OUTER, h, d, :, :, cols],
                bulk_half.at[wave, 0],
                bulk_full.at[wave, 0],
                y,
                along_y,
            )
            own2, own2_on, own2_end = two_way(
                1,
                lambda d, h: tsum.at[OWN, h, :, d, :, cols],
                bulk_half.at[wave, 1],
                bulk_full.at[wave, 1],
                x,
                along_x,
            )
            outer1 = ring(
                2,
                lambda d: tsum.at[OUTER, :, y, lax.rem(x + d, 4), :, cols],
                small_outer,
                along_x,
                4,
            )

            def to_yz(d):
                place = lax.rem(places[1] + d, 8)
                return tsum.at[OWN, place // 4, lax.rem(place, 4), x, :, cols]

            own1 = ring(3, to_yz, small_own, along_yz, 8)
            across = [
                copy(
                    tsum.at[OUTER, q, y, x, :, cols],
                    crossed.at[zl],
                    rz_s.at[wave, q],
                    rz_r.at[wave, zl],
                    {"zl": q, "zh": far, "core": 1 - core},
                )
                for q in range(2)
            ]
            onto = copy(
                tsum.at[OTHER, :, :, :, :, cols],
                otherbuf.at[wave],
                rother_s.at[wave],
                rother_r.at[wave],
                {"core": 1 - core},
            )

            def outer_first():
                outer2_end()
                begin(outer1)

            def own_first():
                own2_end()
                begin(own1)

            def outer_across():
                arrived(outer1)
                tsum[OUTER, :, y, x, :, cols] += small_outer[0] + (
                    small_outer[1] + small_outer[2]
                )
                begin(across)

            def own_done():
                arrived(own1)
                image[:, cols] = tsum[OWN, zl, y, x, :, cols] + jnp.sum(small_own[...], axis=0)

            def collect():
                for q in range(2):
                    copy(
                        tsum.at[OUTER, q, y, x, :, cols],
                        crossed.at[q],
                        rz_s.at[wave, q],
                        rz_r.at[wave, q],
                        {"zl": 1 - zl},
                    ).wait_recv()
                image[:, cols] += crossed[0] + crossed[1]

            return {
                "outer2": lambda: begin(outer2),
                "own2": lambda: begin(own2),
                "other": lambda: begin([onto]),
                "take": onto.wait_recv,
                "outer2_on": outer2_on,
                "own2_on": own2_on,
                "outer1": outer_first,
                "own1": own_first,
                "across": outer_across,
                "own": own_done,
                "collect": collect,
            }

        return [wave_steps(w) for w in range(WAVES)], sends

    class Reduction:
        def __init__(self, k, tile):
            self.k, self.stage = k, 0
            self.send(tile)

        def send(self, tile):
            stage, place = self.stage, places[self.stage]
            self.buf = arbuf.at[self.k, stage]
            self.buf[place] = tile
            mine = self.buf.at[place]
            for d in range(1, sizes[stage]):
                copy(
                    mine,
                    mine,
                    ar_s.at[self.k, stage],
                    ar_r.at[self.k, stage],
                    peers[stage](d),
                ).start()

        def step(self):
            stage, n = self.stage, sizes[self.stage]
            many = self.buf.at[pl.ds(0, n - 1)]
            waited = copy(
                many, many, ar_s.at[self.k, stage], ar_r.at[self.k, stage], peers[stage](1)
            )
            waited.wait_recv()
            waited.wait_send()
            tile = jnp.sum(self.buf[pl.ds(0, n)], axis=0)
            self.stage += 1
            if self.stage < 3:
                self.send(tile)
            return tile

    def packed(*values):
        row = lax.broadcasted_iota(jnp.int32, TILE, 0)
        tile = jnp.zeros(TILE, F32)
        for k, value in enumerate(values):
            tile = jnp.where(row == k, value, tile)
        return tile

    def prepare():
        for p in range(PAIRS):
            for c in loads[p]:
                c.wait()

        @pl.loop(0, PAIRS * 4)
        def _(step):
            p = step // 4
            at = pl.multiple_of(lax.rem(step, 4) * 128, 128)
            at2 = pl.multiple_of(at + M, 128)
            at3 = pl.multiple_of(at + 2 * M, 128)
            rows = pl.ds(at, 128)
            left_rows, right_rows = raw[0, p, rows, :], raw[1, p, rows, :]
            hi, lo = split(left_rows)
            lcat[p, rows, 0:M] = hi
            lcat[p, rows, M : 2 * M] = hi
            lcat[p, rows, 2 * M :] = lo
            hi, lo = split(left_rows.T)
            ltcat[p, :, rows] = hi
            ltcat[p, :, pl.ds(at2, 128)] = hi
            ltcat[p, :, pl.ds(at3, 128)] = lo
            hi, lo = split(right_rows)
            rcat[p, rows, :] = hi
            rcat[p, pl.ds(at2, 128), :] = hi
            rcat[p, pl.ds(at3, 128), :] = lo
            hi, lo = split(right_rows.T)
            for third, part in enumerate((hi, hi, lo)):
                rtcat[p, third * M : (third + 1) * M, rows] = part

    def halve(app, role, wave):
        cols = pl.ds(wave * CW, CW)

        @pl.loop(0, 8)
        def _(step):
            h, j = step // 4, lax.rem(step, 4)
            at = pl.multiple_of(step * 64, 64)
            hi, lo = split(v[app, role, h, j, :, :, cols].reshape(64, CW))
            vcat[role, pl.ds(at, 64), cols] = hi
            vcat[role, pl.ds(pl.multiple_of(at + M, 64), 64), cols] = lo
            vcat[role, pl.ds(pl.multiple_of(at + 2 * M, 64), 64), cols] = hi

    def first_products(wave, forward):
        cols = pl.ds(wave * CW, CW)
        for p in range(PAIRS):
            if forward:
                hi, lo = split(dot(lcat[p], vcat[OWN, :, cols]))
                into = ycat
            else:
                hi, lo = split(weights[p] * dot(ltcat[p], vcat[roles[p], :, cols]))
                into = zcat
            for third, part in enumerate((hi, lo, hi)):
                into[p, :, third * M + wave * CW : third * M + (wave + 1) * CW] = part

    def forward_terms(app, wave):
        cols = pl.ds(wave * CW, CW)
        for p in range(PAIRS):
            fbuf[p] = dot(ycat[p], rtcat[p, :, cols])
        factors = [
            [jnp.where(roles[p] == r, weights[p], 0.0) for p in range(PAIRS)] for r in range(3)
        ]

        def body(step, acc):
            h, j = step // 4, lax.rem(step, 4)
            rows = pl.ds(pl.multiple_of(step * 64, 64), 64)
            f = [fbuf[p, rows, :] for p in range(PAIRS)]
            for r in range(3):
                term = factors[r][0] * f[0] + factors[r][1] * f[1] + factors[r][2] * f[2]
                tsum[r, h, j, :, :, cols] = term.reshape(4, ROWS, CW)
                both = term * v[app, r, h, j, :, :, cols].reshape(64, CW)
                acc = acc + jnp.sum(both.reshape(8, 8, CW), axis=0)
            return acc

        return lax.fori_loop(0, 8, body, jnp.zeros((8, CW), F32))

    def backward_terms(wave):
        cols = pl.ds(wave * CW, CW)
        for p in range(PAIRS):
            fbuf[p] = dot(zcat[p], rcat[p, :, cols])

    def join(wave):
        cols = pl.ds(wave * CW, CW)

        @pl.loop(0, 8)
        def _(step):
            h, j = step // 4, lax.rem(step, 4)
            rows = pl.ds(pl.multiple_of(step * 64, 64), 64)
            back = fbuf[0, rows, :] + fbuf[1, rows, :] + fbuf[2, rows, :]
            tsum[OWN, h, j, :, :, cols] += (
                back.reshape(4, ROWS, CW) + otherbuf[wave, h, j]
            )

    def apply(app, source, scalars):
        v[app, OWN, zl, y, x] = source
        waves, gather_sends = gathering(app)
        for step in ("across", "own1"):
            for g in waves:
                g[step]()
        values = scalars()
        beside = Reduction(1, packed(*values)) if app else None
        for g in waves:
            g["outer1"]()
        for g in waves:
            g["own2"]()
        for g in waves:
            g["outer2"]()
        for g in waves:
            g["own2_on"]()
            g["outer2_on"]()
        if beside:
            beside.step()
        for w, g in enumerate(waves):
            g["own"]()
            halve(app, OWN, w)
            first_products(w, True)
        if beside:
            beside.step()
        for w, g in enumerate(waves):
            g["other"]()
            halve(app, OTHER, w)
            g["outer"]()
            halve(app, OUTER, w)
            first_products(w, False)
        beside = beside.step() if beside else None
        waves, sum_sends = summing(app)
        parts = []
        for w, g in enumerate(waves):
            parts.append(forward_terms(app, w))
            g["other"]()
            g["outer2"]()
            if w == WAVES - 1:
                partial = 2.0 * sum(total(part) for part in parts)
                full = Reduction(2 * app, packed(partial, *(() if app else values)))
            backward_terms(w)
            g["take"]()
            join(w)
            g["own2"]()
            if w:
                waves[w - 1]["outer2_on"]()
                waves[w - 1]["own2_on"]()
        waves[-1]["outer2_on"]()
        waves[-1]["own2_on"]()
        full.step()
        for g in waves[:-1]:
            g["outer1"]()
            g["own1"]()
        waves[-1]["outer1"]()
        waves[-1]["own1"]()
        full.step()
        for g in waves:
            g["across"]()
        for g in waves:
            g["own"]()
        result = full.step()
        for g in waves:
            g["collect"]()
        for c in gather_sends + sum_sends:
            c.wait_send()
        return result, beside

    prepare()
    pl.semaphore_wait(barrier, len(signals))
    w = w_in[...]
    sums, _ = apply(0, w, lambda: (total(w * w),))
    correlation, norm_sq = sums[0:1, 0:1], sums[1:2, 0:1]
    theta = correlation / norm_sq
    inverse = lax.rsqrt(norm_sq)
    vector = w * inverse
    first = image[...] * inverse
    correction = (first - theta * vector) / pre_in[...]
    corrected[...] = correction
    held[...] = first
    sums, beside = apply(
        1,
        correction,
        lambda: (
            total(vector * correction),
            total(correction * correction),
            total(first * correction),
        ),
    )
    product = sums[0:1, 0:1]
    along, squared, with_image = beside[0:1, 0:1], beside[1:2, 0:1], beside[2:3, 0:1]
    length_sq = squared - along * along
    scale_back = lax.rsqrt(length_sq + 1e-30)
    corner = (
        scale_back * scale_back * (product - 2.0 * along * with_image + along * along * theta)
    )
    cross = scale_back * (with_image - along * theta)
    half = (theta - corner) / 2.0
    lowest = (theta + corner) / 2.0 - jnp.sqrt(half * half + cross * cross)
    u1 = corner - lowest
    u2 = -cross
    size_norm = jnp.sqrt(u1 * u1 + u2 * u2 + 1e-30)
    scale = math.sqrt(8 * M * M)
    one, two = scale * u1 / size_norm, scale * u2 / size_norm
    vector = w_in[...] * inverse
    first = held[...]
    basis = (corrected[...] - along * vector) * scale_back
    second = (image[...] - along * first) * scale_back
    packed_out[0:ROWS, :] = one * vector + two * basis
    packed_out[ROWS : 2 * ROWS, :] = one * first + two * second
    packed_out[2 * ROWS :, 0:128] = packed(theta, lowest)


def per_device(wavefunction, preconditioner, left_ops, right_ops, charges, coupling):
    vmem = pl.BlockSpec(memory_space=pltpu.VMEM)
    smem = pl.BlockSpec(memory_space=pltpu.SMEM)
    dma = pltpu.SemaphoreType.DMA
    out = pl.pallas_call(
        kernel,
        out_shape=jax.ShapeDtypeStruct((2 * ROWS + 8, M), F32),
        in_specs=[smem, smem, vmem, vmem]
        + [pl.BlockSpec(memory_space=pl.ANY)] * 2,
        out_specs=vmem,
        scratch_shapes=[
            pltpu.VMEM((2, PAIRS, M, M), F32),
            pltpu.VMEM((PAIRS, M, 3 * M), BF16),
            pltpu.VMEM((PAIRS, M, 3 * M), BF16),
            pltpu.VMEM((PAIRS, 3 * M, M), BF16),
            pltpu.VMEM((PAIRS, 3 * M, M), BF16),
            pltpu.VMEM((2, 3, 2, 4, 4, ROWS, M), F32),
            pltpu.VMEM((3, 3 * M, M), BF16),
            pltpu.VMEM((PAIRS, M, 3 * M), BF16),
            pltpu.VMEM((PAIRS, M, 3 * M), BF16),
            pltpu.VMEM((PAIRS, M, CW), F32),
            pltpu.VMEM((3, 2, 4, 4, ROWS, M), F32),
            pltpu.VMEM((WAVES, 2, 4, 4, ROWS, CW), F32),
            pltpu.VMEM((WAVES, 2, 2, 4, ROWS, CW), F32),
            pltpu.VMEM((WAVES, 2, 2, 2, 4, ROWS, CW), F32),
            pltpu.VMEM((WAVES, 3, 2, ROWS, CW), F32),
            pltpu.VMEM((WAVES, 7, ROWS, CW), F32),
            pltpu.VMEM((WAVES, 2, ROWS, CW), F32),
            pltpu.VMEM((ROWS, M), F32),
            pltpu.VMEM((ROWS, M), F32),
            pltpu.VMEM((ROWS, M), F32),
            pltpu.VMEM((3, 3, 8) + TILE, F32),
            dma((2, PAIRS)),
            dma((WAVES, 2)),
            dma((WAVES, 2)),
            dma((WAVES, 4, 7)),
            dma((WAVES, 4, 7)),
            dma((WAVES,)),
            dma((WAVES,)),
            dma((WAVES, 2)),
            dma((WAVES, 2)),
            dma((WAVES, 4, 7)),
            dma((WAVES, 4, 7)),
            dma((WAVES,)),
            dma((WAVES,)),
            dma((3, 3)),
            dma((3, 3)),
        ],
        compiler_params=pltpu.CompilerParams(
            collective_id=0, has_side_effects=True, vmem_limit_bytes=60 * 1024 * 1024
        ),
    )(
        charges,
        coupling,
        wavefunction.reshape(ROWS, M),
        preconditioner.reshape(ROWS, M),
        left_ops.reshape(PAIRS, M, M),
        right_ops.reshape(PAIRS, M, M),
    )
    return out[None, 0:ROWS], out[None, ROWS : 2 * ROWS], out[2 * ROWS : 2 * ROWS + 2, 0]


def solution(mesh):
    split_mesh = Mesh(mesh.devices.reshape(2, 4, 4, 4, 2), PAIR + SECTOR)
    placed = (
        P(SECTOR, PAIR, None),
        P(SECTOR, PAIR, None),
        P(PAIR, SECTOR, None, None),
        P(PAIR, SECTOR, None, None),
        P(PAIR),
        P(SECTOR, None),
    )
    return jax.shard_map(
        per_device,
        mesh=split_mesh,
        in_specs=placed,
        out_specs=(P(SECTOR, PAIR, None), P(SECTOR, PAIR, None), P()),
        check_vma=False,
    )
```

time: 135 us -> 117 us (0.87)
  Pallas kernels: 130 us -> 113 us
    pallas_call x1, Pallas kernels: 130 us -> 113 us  [per_device(): pl.pallas_call(kernel, out_shape=jax.ShapeDtypeStruct((2 * ROWS + 8, M),...]
    unnamed x2 -> x0, local copies, waits for them, and re-layouts: 2.75 us -> none
    broadcast_in_dim x0 -> x1, local copies, waits for them, and re-layouts: none -> 1.41 us  [per_device(): out[None, ROWS:2 * ROWS]]
where the time goes in v2:
time: 117 us; the launch traced here: 116 us
  Pallas kernels  113 us (97%)
  local copies, waits for them, and re-layouts  2.7 us (2%)
    pallas_call x1, Pallas kernels, per_device(): pl.pallas_call(kernel, out_shape=jax.ShapeDtypeStruct((2 * ROWS + 8, M),...  113 us

profile of v2, /device:TPU:1, one launch (start us, length us, event | category | flops | bytes accessed | tf_op | source)
XLA Modules:
  0.0 116.5 jit_solution(6855276216604869325)
XLA Ops:
  0.6 113.1 %shard_map.85 = f32[40,512]{1,0:T(8,128)} custom-call(s32[3]{0:T(128)} %charges.1, s32[1,3]{1,0:T(1,128)} %coupling.1, f32[16,512]{1,0:T(8,128)} %bitcast.10, f32[16,512]{1,0:T(8,128)} %bitcast.11, f32[3,512,512]{2,1,0:T(8,128)} %bitcast.8, f32[3,512,512]{2,1,0:T(8,128)} %bitcast.9), custom_call_target="tpu_custom_call" | custom-call | tf_op jit(solution)/shard_map/pallas_call | solution.py:652
  113.8 1.4 %slice_bitcast_fusion = (f32[1,16,512]{2,1,0:T(8,128)}, f32[1,16,512]{2,1,0:T(8,128)}) fusion(f32[40,512]{1,0:T(8,128)} %shard_map.85), kind=kLoop, calls=%fused_computation | loop fusion | bytes 131072 | tf_op jit(solution)/shard_map/broadcast_in_dim | solution.py:707
  115.2 1.3 %slice_reduce_fusion = f32[2]{0:T(128)} fusion(f32[40,512]{1,0:T(8,128)} %shard_map.85), kind=kLoop, calls=%fused_computation.2 | loop fusion | bytes 16 | tf_op jit(solution)/shard_map/slice | solution.py:707

commit v3 on v2

--- a/solution.py
+++ b/solution.py
@@ -18,7 +18,7 @@
 ROWS = 16
 PAIRS = 3
 OUTER, OWN, OTHER = 0, 1, 2
-WAVES = 2
+WAVES = 1
 CW = M // WAVES
 TILE = (8, 128)
 
@@ -86,20 +86,24 @@
     far = lax.rem(zh + 2 * core + 3, 4)
     places = (x, zl * 4 + y, zh * 2 + core)
     sizes = (4, 8, 8)
+    away = [{"zl": q, "zh": far, "core": 1 - core} for q in range(2)]
+    partner = {"core": 1 - core}
+    in_x = [{"x": (x + d) & 3} for d in range(4)]
+    in_y = [{"y": (y + d) & 3} for d in range(4)]
+    in_yz = [{"zl": ((places[1] + d) & 7) >> 2, "y": (places[1] + d) & 3} for d in range(8)]
+    in_sector = [{"zh": ((places[2] + d) & 7) >> 1, "core": (places[2] + d) & 1} for d in range(8)]
 
     def along_x(d):
-        return {"x": lax.rem(x + d, 4)}
+        return in_x[d]
 
     def along_y(d):
-        return {"y": lax.rem(y + d, 4)}
+        return in_y[d]
 
     def along_yz(d):
-        place = lax.rem(places[1] + d, 8)
-        return {"zl": place // 4, "y": lax.rem(place, 4)}
+        return in_yz[d]
 
     def along_sector(d):
-        place = lax.rem(places[2] + d, 8)
-        return {"zh": place // 2, "core": lax.rem(place, 2)}
+        return in_sector[d]
 
     peers = (along_x, along_yz, along_sector)
 
@@ -154,8 +158,8 @@
                     copy(
                         ref,
                         ref,
-                        ring_s.at[wave, phase, d - 1],
-                        ring_r.at[wave, phase, d - 1],
+                        ring_s.at[app, wave, phase, d - 1],
+                        ring_r.at[app, wave, phase, d - 1],
                         group(d),
                     )
                     for d in range(1, n)
@@ -165,9 +169,9 @@
                 copy(
                     mine,
                     block.at[OUTER, zl, y, x, :, cols],
-                    z_s.at[wave, q],
-                    z_r.at[wave, zl],
-                    {"zl": q, "zh": far, "core": 1 - core},
+                    z_s.at[app, wave, q],
+                    z_r.at[app, wave, zl],
+                    away[q],
                 )
                 for q in range(2)
             ]
@@ -177,7 +181,7 @@
             def two_way(phase, unit, i, group):
                 def one(ref, d, k):
                     return copy(
-                        ref, ref, ring_s.at[wave, phase, k], ring_r.at[wave, phase, k], group(d)
+                        ref, ref, ring_s.at[app, wave, phase, k], ring_r.at[app, wave, phase, k], group(d)
                     )
 
                 first = [
@@ -199,9 +203,9 @@
             onto = copy(
                 block.at[OWN, :, :, :, :, cols],
                 block.at[OTHER, :, :, :, :, cols],
-                other_s.at[wave],
-                other_r.at[wave],
-                {"core": 1 - core},
+                other_s.at[app, wave],
+                other_r.at[app, wave],
+                partner,
             )
 
             def arrived(copies):
@@ -212,7 +216,7 @@
                 for q in range(2):
                     there = block.at[OUTER, q, y, x, :, cols]
                     copy(
-                        there, there, z_s.at[wave, q], z_r.at[wave, q], {"zl": 1 - zl}
+                        there, there, z_s.at[app, wave, q], z_r.at[app, wave, q], away[q]
                     ).wait_recv()
                 begin(outer1)
 
@@ -268,18 +272,18 @@
                     copy(
                         chunk(d),
                         into.at[d - 1],
-                        rring_s.at[wave, phase, d - 1],
-                        rring_r.at[wave, phase, d - 1],
+                        rring_s.at[app, wave, phase, d - 1],
+                        rring_r.at[app, wave, phase, d - 1],
                         group(d),
                     )
                     for d in range(1, n)
                 ]
 
-            small_outer, small_own, crossed = tail3.at[wave], tail7.at[wave], tail2.at[wave]
+            small_outer, small_own, crossed = tail3.at[wave], tail7.at[wave], tail2.at[app, wave]
             def two_way(phase, chunk, half, full, i, group):
                 def one(src, dst, d, k):
                     return copy(
-                        src, dst, rring_s.at[wave, phase, k], rring_r.at[wave, phase, k], group(d)
+                        src, dst, rring_s.at[app, wave, phase, k], rring_r.at[app, wave, phase, k], group(d)
                     )
 
                 right, left, opposite = lax.rem(i + 1, 4), lax.rem(i + 3, 4), lax.rem(i + 2, 4)
@@ -341,18 +345,18 @@
                 copy(
                     tsum.at[OUTER, q, y, x, :, cols],
                     crossed.at[zl],
-                    rz_s.at[wave, q],
-                    rz_r.at[wave, zl],
-                    {"zl": q, "zh": far, "core": 1 - core},
+                    rz_s.at[app, wave, q],
+                    rz_r.at[app, wave, zl],
+                    away[q],
                 )
                 for q in range(2)
             ]
             onto = copy(
                 tsum.at[OTHER, :, :, :, :, cols],
-                otherbuf.at[wave],
-                rother_s.at[wave],
-                rother_r.at[wave],
-                {"core": 1 - core},
+                otherbuf.at[app, wave],
+                rother_s.at[app, wave],
+                rother_r.at[app, wave],
+                partner,
             )
 
             def outer_first():
@@ -379,9 +383,9 @@
                     copy(
                         tsum.at[OUTER, q, y, x, :, cols],
                         crossed.at[q],
-                        rz_s.at[wave, q],
-                        rz_r.at[wave, q],
-                        {"zl": 1 - zl},
+                        rz_s.at[app, wave, q],
+                        rz_r.at[app, wave, q],
+                        away[q],
                     ).wait_recv()
                 image[:, cols] += crossed[0] + crossed[1]
 
@@ -441,15 +445,13 @@
             tile = jnp.where(row == k, value, tile)
         return tile
 
-    def prepare():
-        for p in range(PAIRS):
-            for c in loads[p]:
-                c.wait()
-
-        @pl.loop(0, PAIRS * 4)
+    def prepare(p):
+        for c in loads[p]:
+            c.wait()
+
+        @pl.loop(0, 4)
         def _(step):
-            p = step // 4
-            at = pl.multiple_of(lax.rem(step, 4) * 128, 128)
+            at = pl.multiple_of(step * 128, 128)
             at2 = pl.multiple_of(at + M, 128)
             at3 = pl.multiple_of(at + 2 * M, 128)
             rows = pl.ds(at, 128)
@@ -520,7 +522,7 @@
         for p in range(PAIRS):
             fbuf[p] = dot(zcat[p], rcat[p, :, cols])
 
-    def join(wave):
+    def join(app, wave):
         cols = pl.ds(wave * CW, CW)
 
         @pl.loop(0, 8)
@@ -529,90 +531,111 @@
             rows = pl.ds(pl.multiple_of(step * 64, 64), 64)
             back = fbuf[0, rows, :] + fbuf[1, rows, :] + fbuf[2, rows, :]
             tsum[OWN, h, j, :, :, cols] += (
-                back.reshape(4, ROWS, CW) + otherbuf[wave, h, j]
-            )
-
-    def apply(app, source, scalars):
+                back.reshape(4, ROWS, CW) + otherbuf[app, wave, h, j]
+            )
+
+    def apply(app, source, scalars, settle, then):
         v[app, OWN, zl, y, x] = source
-        waves, gather_sends = gathering(app)
+        gather, gather_sends = gathering(app)
+        summed, sum_sends = summing(app)
         for step in ("across", "own1"):
-            for g in waves:
+            for g in gather:
                 g[step]()
         values = scalars()
-        beside = Reduction(1, packed(*values)) if app else None
-        for g in waves:
-            g["outer1"]()
-        for g in waves:
-            g["own2"]()
-        for g in waves:
-            g["outer2"]()
-        for g in waves:
+        for p, step in enumerate(("outer1", "own2", "outer2")):
+            if app == 0:
+                prepare(p)
+            for g in gather:
+                g[step]()
+        for g in gather:
             g["own2_on"]()
             g["outer2_on"]()
-        if beside:
-            beside.step()
-        for w, g in enumerate(waves):
+        for w, g in enumerate(gather):
             g["own"]()
             halve(app, OWN, w)
             first_products(w, True)
-        if beside:
-            beside.step()
-        for w, g in enumerate(waves):
+        for w, g in enumerate(gather):
             g["other"]()
             halve(app, OTHER, w)
             g["outer"]()
             halve(app, OUTER, w)
             first_products(w, False)
-        beside = beside.step() if beside else None
-        waves, sum_sends = summing(app)
-        parts = []
-        for w, g in enumerate(waves):
-            parts.append(forward_terms(app, w))
-            g["other"]()
-            g["outer2"]()
+        part = jnp.zeros((8, CW), F32)
+        for w, s in enumerate(summed):
+            part += forward_terms(app, w)
+            s["other"]()
+            s["outer2"]()
             if w == WAVES - 1:
-                partial = 2.0 * sum(total(part) for part in parts)
-                full = Reduction(2 * app, packed(partial, *(() if app else values)))
+                full = Reduction(app, packed(2.0 * total(part), *values))
             backward_terms(w)
-            g["take"]()
-            join(w)
-            g["own2"]()
+            s["take"]()
+            join(app, w)
+            s["own2"]()
             if w:
-                waves[w - 1]["outer2_on"]()
-                waves[w - 1]["own2_on"]()
-        waves[-1]["outer2_on"]()
-        waves[-1]["own2_on"]()
+                summed[w - 1]["outer2_on"]()
+                summed[w - 1]["own2_on"]()
+        summed[-1]["outer2_on"]()
+        summed[-1]["own2_on"]()
         full.step()
-        for g in waves[:-1]:
-            g["outer1"]()
-            g["own1"]()
-        waves[-1]["outer1"]()
-        waves[-1]["own1"]()
+        for s in summed:
+            s["outer1"]()
+            s["own1"]()
         full.step()
-        for g in waves:
-            g["across"]()
-        for g in waves:
-            g["own"]()
-        result = full.step()
-        for g in waves:
-            g["collect"]()
+        for s in summed:
+            s["across"]()
+        for s in summed:
+            s["own"]()
+        then(full.step())
+        for s in summed:
+            s["collect"]()
         for c in gather_sends + sum_sends:
             c.wait_send()
-        return result, beside
-
-    prepare()
+        return []
+
     pl.semaphore_wait(barrier, len(signals))
     w = w_in[...]
-    sums, _ = apply(0, w, lambda: (total(w * w),))
-    correlation, norm_sq = sums[0:1, 0:1], sums[1:2, 0:1]
-    theta = correlation / norm_sq
-    inverse = lax.rsqrt(norm_sq)
+    known = {}
+
+    def first_sums(sums):
+        correlation, norm_sq = sums[0:1, 0:1], sums[1:2, 0:1]
+        known["theta"] = correlation / norm_sq
+        known["inverse"] = lax.rsqrt(norm_sq)
+
+    sends = apply(0, w, lambda: (total(w * w),), lambda: None, first_sums)
+    theta, inverse = known["theta"], known["inverse"]
     vector = w * inverse
     first = image[...] * inverse
     correction = (first - theta * vector) / pre_in[...]
     corrected[...] = correction
     held[...] = first
-    sums, beside = apply(
+
+    def settle():
+        for c in sends:
+            c.wait_send()
+
+    def second_sums(sums):
+        product, along, squared, with_image = (sums[k : k + 1, 0:1] for k in range(4))
+        length_sq = squared - along * along
+        scale_back = lax.rsqrt(length_sq + 1e-30)
+        corner = (
+            scale_back * scale_back * (product - 2.0 * along * with_image + along * along * theta)
+        )
+        cross = scale_back * (with_image - along * theta)
+        half = (theta - corner) / 2.0
+        lowest = (theta + corner) / 2.0 - jnp.sqrt(half * half + cross * cross)
+        u1 = corner - lowest
+        u2 = -cross
+        size_norm = jnp.sqrt(u1 * u1 + u2 * u2 + 1e-30)
+        scale = math.sqrt(8 * M * M)
+        one, two = scale * u1 / size_norm, scale * u2 / size_norm
+        vector, first = w_in[...] * inverse, held[...]
+        basis = (corrected[...] - along * vector) * scale_back
+        packed_out[0:ROWS, :] = one * vector + two * basis
+        lane = lax.broadcasted_iota(jnp.int32, TILE, 1)
+        packed_out[2 * ROWS :, 0:128] = jnp.where(lane == 0, theta, lowest)
+        known["rest"] = one, two * scale_back, along
+
+    last_sends = apply(
         1,
         correction,
         lambda: (
@@ -620,29 +643,14 @@
             total(correction * correction),
             total(first * correction),
         ),
+        settle,
+        second_sums,
     )
-    product = sums[0:1, 0:1]
-    along, squared, with_image = beside[0:1, 0:1], beside[1:2, 0:1], beside[2:3, 0:1]
-    length_sq = squared - along * along
-    scale_back = lax.rsqrt(length_sq + 1e-30)
-    corner = (
-        scale_back * scale_back * (product - 2.0 * along * with_image + along * along * theta)
-    )
-    cross = scale_back * (with_image - along * theta)
-    half = (theta - corner) / 2.0
-    lowest = (theta + corner) / 2.0 - jnp.sqrt(half * half + cross * cross)
-    u1 = corner - lowest
-    u2 = -cross
-    size_norm = jnp.sqrt(u1 * u1 + u2 * u2 + 1e-30)
-    scale = math.sqrt(8 * M * M)
-    one, two = scale * u1 / size_norm, scale * u2 / size_norm
-    vector = w_in[...] * inverse
+    one, two, along = known["rest"]
     first = held[...]
-    basis = (corrected[...] - along * vector) * scale_back
-    second = (image[...] - along * first) * scale_back
-    packed_out[0:ROWS, :] = one * vector + two * basis
-    packed_out[ROWS : 2 * ROWS, :] = one * first + two * second
-    packed_out[2 * ROWS :, 0:128] = packed(theta, lowest)
+    packed_out[ROWS : 2 * ROWS, :] = one * first + two * (image[...] - along * first)
+    for c in last_sends:
+        c.wait_send()
 
 
 def per_device(wavefunction, preconditioner, left_ops, right_ops, charges, coupling):
@@ -667,31 +675,31 @@
             pltpu.VMEM((PAIRS, M, 3 * M), BF16),
             pltpu.VMEM((PAIRS, M, CW), F32),
             pltpu.VMEM((3, 2, 4, 4, ROWS, M), F32),
-            pltpu.VMEM((WAVES, 2, 4, 4, ROWS, CW), F32),
+            pltpu.VMEM((2, WAVES, 2, 4, 4, ROWS, CW), F32),
             pltpu.VMEM((WAVES, 2, 2, 4, ROWS, CW), F32),
             pltpu.VMEM((WAVES, 2, 2, 2, 4, ROWS, CW), F32),
             pltpu.VMEM((WAVES, 3, 2, ROWS, CW), F32),
             pltpu.VMEM((WAVES, 7, ROWS, CW), F32),
-            pltpu.VMEM((WAVES, 2, ROWS, CW), F32),
+            pltpu.VMEM((2, WAVES, 2, ROWS, CW), F32),
             pltpu.VMEM((ROWS, M), F32),
             pltpu.VMEM((ROWS, M), F32),
             pltpu.VMEM((ROWS, M), F32),
-            pltpu.VMEM((3, 3, 8) + TILE, F32),
+            pltpu.VMEM((2, 3, 8) + TILE, F32),
             dma((2, PAIRS)),
-            dma((WAVES, 2)),
-            dma((WAVES, 2)),
-            dma((WAVES, 4, 7)),
-            dma((WAVES, 4, 7)),
-            dma((WAVES,)),
-            dma((WAVES,)),
-            dma((WAVES, 2)),
-            dma((WAVES, 2)),
-            dma((WAVES, 4, 7)),
-            dma((WAVES, 4, 7)),
-            dma((WAVES,)),
-            dma((WAVES,)),
-            dma((3, 3)),
-            dma((3, 3)),
+            dma((2, WAVES, 2)),
+            dma((2, WAVES, 2)),
+            dma((2, WAVES, 4, 7)),
+            dma((2, WAVES, 4, 7)),
+            dma((2, WAVES,)),
+            dma((2, WAVES,)),
+            dma((2, WAVES, 2)),
+            dma((2, WAVES, 2)),
+            dma((2, WAVES, 4, 7)),
+            dma((2, WAVES, 4, 7)),
+            dma((2, WAVES,)),
+            dma((2, WAVES,)),
+            dma((2, 3)),
+            dma((2, 3)),
         ],
         compiler_params=pltpu.CompilerParams(
             collective_id=0, has_side_effects=True, vmem_limit_bytes=60 * 1024 * 1024
@@ -704,7 +712,7 @@
         left_ops.reshape(PAIRS, M, M),
         right_ops.reshape(PAIRS, M, M),
     )
-    return out[None, 0:ROWS], out[None, ROWS : 2 * ROWS], out[2 * ROWS : 2 * ROWS + 2, 0]
+    return out[None, 0:ROWS], out[None, ROWS : 2 * ROWS], out[2 * ROWS, 0:2]
 
 
 def solution(mesh):

time: 117 us -> 116 us (level)
    slice x1 -> x0, local copies, waits for them, and re-layouts: 1.3 us -> none  [per_device(): out[2 * ROWS:2 * ROWS + 2, 0]]
    squeeze x0 -> x1, local copies, waits for them, and re-layouts: none -> 1.19 us  [per_device(): return (out[None, 0:ROWS], out[None, ROWS:2 * ROWS], out[2 * ROWS, 0:2])]
where the time goes in v3:
time: 116 us; the launch traced here: 115 us
  Pallas kernels  112 us (97%)
  local copies, waits for them, and re-layouts  2.59 us (2%)
    pallas_call x1, Pallas kernels, per_device(): pl.pallas_call(kernel, out_shape=jax.ShapeDtypeStruct((2 * ROWS + 8, M),...  112 us

profile of v3, /device:TPU:1, one launch (start us, length us, event | category | flops | bytes accessed | tf_op | source)
XLA Modules:
  0.0 115.5 jit_solution(17374229578465121715)
XLA Ops:
  0.6 112.2 %shard_map.85 = f32[40,512]{1,0:T(8,128)} custom-call(s32[3]{0:T(128)} %charges.1, s32[1,3]{1,0:T(1,128)} %coupling.1, f32[16,512]{1,0:T(8,128)} %bitcast.12, f32[16,512]{1,0:T(8,128)} %bitcast.13, f32[3,512,512]{2,1,0:T(8,128)} %bitcast.10, f32[3,512,512]{2,1,0:T(8,128)} %bitcast.11), custom_call_target="tpu_custom_call" | custom-call | tf_op jit(solution)/shard_map/pallas_call | solution.py:660
  112.9 1.4 %slice_bitcast_fusion = (f32[1,16,512]{2,1,0:T(8,128)}, f32[1,16,512]{2,1,0:T(8,128)}) fusion(f32[40,512]{1,0:T(8,128)} %shard_map.85), kind=kLoop, calls=%fused_computation | loop fusion | bytes 131072 | tf_op jit(solution)/shard_map/broadcast_in_dim | solution.py:715
  114.3 1.2 %slice_bitcast_fusion.2 = f32[2]{0:T(128)} fusion(f32[40,512]{1,0:T(8,128)} %shard_map.85), kind=kLoop, calls=%fused_computation.2 | loop fusion | bytes 16 | tf_op jit(solution)/shard_map/squeeze | solution.py:715

commit v4 on v3

--- a/solution.py
+++ b/solution.py
@@ -565,12 +565,12 @@
             part += forward_terms(app, w)
             s["other"]()
             s["outer2"]()
-            if w == WAVES - 1:
-                full = Reduction(app, packed(2.0 * total(part), *values))
             backward_terms(w)
             s["take"]()
             join(app, w)
             s["own2"]()
+            if w == WAVES - 1:
+                full = Reduction(app, packed(2.0 * total(part), *values))
             if w:
                 summed[w - 1]["outer2_on"]()
                 summed[w - 1]["own2_on"]()
@@ -583,12 +583,14 @@
         full.step()
         for s in summed:
             s["across"]()
+        for c in gather_sends:
+            c.wait_send()
         for s in summed:
             s["own"]()
         then(full.step())
         for s in summed:
             s["collect"]()
-        for c in gather_sends + sum_sends:
+        for c in sum_sends:
             c.wait_send()
         return []
 

time: 116 us -> 117 us (level)
  Pallas kernels: 112 us -> 114 us
    pallas_call x1, Pallas kernels: 112 us -> 114 us  [per_device(): pl.pallas_call(kernel, out_shape=jax.ShapeDtypeStruct((2 * ROWS + 8, M),...]
where the time goes in v4:
time: 117 us
  Pallas kernels  114 us (97%)
  local copies, waits for them, and re-layouts  2.59 us (2%)
    pallas_call x1, Pallas kernels, per_device(): pl.pallas_call(kernel, out_shape=jax.ShapeDtypeStruct((2 * ROWS + 8, M),...  114 us

profile of v4, /device:TPU:1, one launch (start us, length us, event | category | flops | bytes accessed | tf_op | source)
XLA Modules:
  0.0 117.2 jit_solution(4555385046095031993)
XLA Ops:
  0.6 114.0 %shard_map.85 = f32[40,512]{1,0:T(8,128)} custom-call(s32[3]{0:T(128)} %charges.1, s32[1,3]{1,0:T(1,128)} %coupling.1, f32[16,512]{1,0:T(8,128)} %bitcast.12, f32[16,512]{1,0:T(8,128)} %bitcast.13, f32[3,512,512]{2,1,0:T(8,128)} %bitcast.10, f32[3,512,512]{2,1,0:T(8,128)} %bitcast.11), custom_call_target="tpu_custom_call" | custom-call | tf_op jit(solution)/shard_map/pallas_call | solution.py:662
  114.6 1.4 %slice_bitcast_fusion = (f32[1,16,512]{2,1,0:T(8,128)}, f32[1,16,512]{2,1,0:T(8,128)}) fusion(f32[40,512]{1,0:T(8,128)} %shard_map.85), kind=kLoop, calls=%fused_computation | loop fusion | bytes 131072 | tf_op jit(solution)/shard_map/broadcast_in_dim | solution.py:717
  116.0 1.2 %slice_bitcast_fusion.2 = f32[2]{0:T(128)} fusion(f32[40,512]{1,0:T(8,128)} %shard_map.85), kind=kLoop, calls=%fused_computation.2 | loop fusion | bytes 16 | tf_op jit(solution)/shard_map/squeeze | solution.py:717
